TPU v7x, 32 devices: a whole 2x2x4 slice. The times are simulated.
32 devices in a mesh: grp: 4 (over y, x), blk: 8 (over z, core).
Axes of the slice: x: 2, y: 2, z: 4, core: 2. Of those that a mesh axis runs over, the one named last changes fastest.
Arguments:
- activations: bfloat16 [32768, 3072], P(('grp', 'blk')), may hold values from -6 to 6
- out_grads: bfloat16 [32768, 3072], P(('grp', 'blk')), may hold values from -6 to 6
- proj_act: bfloat16 [3072, 128], replicated, may hold values from -1 to 1
- proj_out: bfloat16 [3072, 256], replicated, may hold values from -0.109375 to 0.109375
Outputs:
- scores: float32 [512, 128], P(('grp', 'blk'))
All inputs are finite; a program needn't handle non-finite values.
Results may differ from a plain program's by a relative error of at most 0.0012.
Values may be sent and summed in bfloat16 or wider, within the bound.
A program may use at most 128 MiB of HBM per device.

v0:
```python
import functools
import math

import jax
import jax.numpy as jnp
from jax import lax
from jax.experimental import pallas as pl
from jax.experimental.pallas import tpu as pltpu
from jax.sharding import PartitionSpec as P

SEQ = 64
ITERS = 4
damping_rate = 0.5
power_steps = 3
MESH = pl.DeviceIdType.MESH
NT = (((1,), (1,)), ((), ()))
TN = (((0,), (0,)), ((), ()))


def mix_kernel(
    groups, blocks, examples, ranks, width,
    act_ref, grad_ref, out_ref,
    wide, feat_ref, stat_ref, recv, stats, part, landed, packs, full, prow_part, prow_land, row, col, col_next,
    y_ref, sc, sc_land,
    f_send, f_recv, t_send, t_recv, r_send, r_recv, g_send, g_recv, p_send, p_recv, s_send, s_recv,
):
    devices = groups * blocks
    group_ex = examples * blocks
    total_ex = group_ex * groups
    span = recv.shape[2]
    rows_out = ranks * examples
    grp, blk = lax.axis_index("grp"), lax.axis_index("blk")
    me = grp * blocks + blk

    half = blocks // 2 * groups

    def peer_of(d):
        pg = lax.rem(grp + lax.rem(d, groups), groups)
        pb = lax.rem(blk + blocks // 2 + d // groups, blocks)
        return pg * blocks + pb, pg, pb

    def over_peers(step):
        lax.fori_loop(0, half, step, 0)
        lax.fori_loop(half + 1, devices, step, 0)

    barrier = pltpu.get_barrier_semaphore()

    def greet(d, c):
        _, pg, pb = peer_of(d)
        pl.semaphore_signal(barrier, inc=1, device_id=(pg, pb), device_id_type=MESH)
        return c

    over_peers(greet)
    for e in range(examples):
        tokens = pl.ds(e * SEQ, SEQ)
        product = lax.dot_general(
            act_ref[tokens, :], grad_ref[tokens, :], TN, preferred_element_type=jnp.float32
        )
        for c in range(wide.shape[0]):
            wide[c, pl.ds(e, act_ref.shape[1], stride=examples), :] = (
                product[:, c * 128:(c + 1) * 128])
    stat_ref[...] = jnp.zeros_like(stat_ref)
    pl.semaphore_wait(barrier, devices - 1)

    def feature_copy(dest, pg, pb, slot):
        return pltpu.make_async_remote_copy(
            src_ref=feat_ref.at[pb * groups + pg], dst_ref=recv.at[slot],
            send_sem=f_send.at[dest], recv_sem=f_recv.at[slot],
            device_id=(pg, pb), device_id_type=MESH)

    def stat_copy(dest, pg, pb, slot):
        return pltpu.make_async_remote_copy(
            src_ref=stat_ref, dst_ref=stats.at[slot],
            send_sem=t_send.at[dest], recv_sem=t_recv.at[slot],
            device_id=(pg, pb), device_id_type=MESH)

    def narrow(pg, pb):
        slot = pb * groups + pg
        rows = pl.ds(pl.multiple_of(slot * rows_out, rows_out), rows_out)
        for c in range(wide.shape[0]):
            low = wide[c, rows, :].astype(jnp.bfloat16)
            feat_ref[slot, :, c * 128:(c + 1) * 128] = low
            back = low.astype(jnp.float32)
            square = jnp.sum(back * back, axis=0, keepdims=True)
            stat_ref[...] += jnp.broadcast_to(square, stat_ref.shape)

    def send(d, c):
        peer, pg, pb = peer_of(d)
        narrow(pg, pb)
        feature_copy(peer, pg, pb, me).start()
        return c

    over_peers(send)
    narrow(grp, blk)
    recv[me] = feat_ref[blk * groups + grp]

    def send_stat(d, c):
        peer, pg, pb = peer_of(d)
        stat_copy(peer, pg, pb, me).start()
        return c

    over_peers(send_stat)
    stats[me] = stat_ref[...]

    def arrive(d, c):
        peer, pg, pb = peer_of(d)
        feature_copy(peer, pg, pb, peer).wait_recv()
        return c

    over_peers(arrive)

    def grp_rows(h):
        return pl.ds(pl.multiple_of(h * group_ex, group_ex), group_ex)

    split = groups % 2 == 0
    whole_blocks = (groups - 1) // 2 + 1
    pair = groups // 2
    half_ex = group_ex // 2

    def block_into(h, at, left_at, left_n, right_at):
        for r in range(ranks):
            here = pl.ds(r * examples, examples)
            left = recv[pl.ds(left_at, left_n), here, :].reshape(left_n * examples, span)
            right = recv[pl.ds(right_at, blocks), here, :].reshape(group_ex, span)
            term = lax.dot_general(left, right, NT, preferred_element_type=jnp.float32)
            if r == 0:
                part[h, at:at + left_n * examples, :] = term
            else:
                part[h, at:at + left_n * examples, :] += term

    def part_of(h, q):
        for d in range(1) if q == 0 else range(1, whole_blocks):
            block_into(h, d * group_ex, h * blocks, blocks, lax.rem(h + d, groups) * blocks)
        if split and q == 1:
            low = lax.rem(h, pair)
            block_into(h, whole_blocks * group_ex,
                       low * blocks + h // pair * (blocks // 2), blocks // 2,
                       (low + pair) * blocks)

    cuts = (slice(0, group_ex), slice(group_ex, part.shape[1]))

    def part_copy(h, d, slot, q):
        return pltpu.make_async_remote_copy(
            src_ref=part.at[h, cuts[q]], dst_ref=landed.at[slot, cuts[q]],
            send_sem=r_send.at[2 * d + q], recv_sem=r_recv.at[2 * slot + q],
            device_id=(h, blk), device_id_type=MESH)

    def full_copy(h, slot, q):
        return pltpu.make_async_remote_copy(
            src_ref=packs.at[slot, cuts[q]], dst_ref=packs.at[slot, cuts[q]],
            send_sem=g_send.at[2 * h + q], recv_sem=g_recv.at[2 * slot + q],
            device_id=(h, blk), device_id_type=MESH)

    def prow_copy(h, slot):
        return pltpu.make_async_remote_copy(
            src_ref=prow_part, dst_ref=prow_land.at[slot],
            send_sem=p_send.at[h], recv_sem=p_recv.at[slot],
            device_id=(h, blk), device_id_type=MESH)

    others = [lax.rem(grp + d, groups) for d in range(1, groups)]

    for q in range(2):
        def part_step(d, c, q=q):
            h = lax.rem(grp + d, groups)
            part_of(h, q)
            part_copy(h, d, groups - d - 1, q).start()
            return c

        lax.fori_loop(1, groups, part_step, 0)
    for q in range(2):
        part_of(grp, q)

    ones = jnp.ones((8, span), jnp.bfloat16)
    scale = 1.0 / math.sqrt(width)
    for c in range(groups):
        cols = slice(c * group_ex, (c + 1) * group_ex)
        acc = jnp.zeros((8, group_ex), jnp.float32)
        for r in range(ranks):
            right = recv[c * blocks:(c + 1) * blocks, pl.ds(r * examples, examples), :]
            acc += lax.dot_general(
                ones, right.reshape(group_ex, span), NT, preferred_element_type=jnp.float32)
        prow_part[:, cols] = acc * scale
    for h in others:
        prow_copy(h, grp).start()

    for q in range(2):
        for d, h in enumerate(others):
            part_copy(h, d + 1, d, q).wait_recv()
        mine = part[grp, cuts[q], :]
        for d in range(groups - 1):
            mine += landed[d, cuts[q], :]
        packs[grp, cuts[q], :] = mine
        for h in others:
            full_copy(h, grp, q).start()

    def arrive_stat(d, c):
        peer, pg, pb = peer_of(d)
        stat_copy(peer, pg, pb, peer).wait_recv()
        return c

    over_peers(arrive_stat)
    total = jnp.sum(jnp.sum(stats[...], axis=0)[:1, :], axis=1, keepdims=True)
    damping = damping_rate * total / (width * blocks)
    for h in others:
        prow_copy(h, h).wait_recv()
    first = prow_part[...]
    for h in others:
        first += prow_land[h]
    row[...] = first
    for h in others:
        for q in range(2):
            full_copy(h, h, q).wait_recv()
    for o in range(groups):
        here = slice(o * group_ex, (o + 1) * group_ex)
        for d in range(whole_blocks):
            there = (o + d) % groups
            there = slice(there * group_ex, (there + 1) * group_ex)
            entry = packs[o, d * group_ex:(d + 1) * group_ex, :]
            full[here, there] = entry
            if d:
                full[there, here] = entry.T
        if split:
            low = o % pair
            start = low * group_ex + o // pair * half_ex
            there = slice((low + pair) * group_ex, (low + pair + 1) * group_ex)
            entry = packs[o, whole_blocks * group_ex:, :]
            full[start:start + half_ex, there] = entry
            full[there, start:start + half_ex] = entry.T

    tile = 128
    tiles = total_ex // tile

    def tile_rows(i):
        return pl.ds(pl.multiple_of(i * tile, tile), tile)

    def turn(i, c):
        spot = lax.broadcasted_iota(jnp.int32, (tile, total_ex), 0) + i * tile
        lane = lax.broadcasted_iota(jnp.int32, (tile, total_ex), 1)
        picked = jnp.where(spot == lane, row[:1, :], 0.0)
        col[tile_rows(i), :] = jnp.broadcast_to(
            jnp.sum(picked, axis=1, keepdims=True), (tile, 128))
        return c

    lax.fori_loop(0, tiles, turn, 0)
    top = None
    for step in range(power_steps):
        last = step + 1 == power_steps
        prow = row[:1, :]

        def image(i, acc):
            k_tile = full[tile_rows(i), :]
            if not last:
                col_next[tile_rows(i), :] = jnp.broadcast_to(
                    jnp.sum(k_tile * prow, axis=1, keepdims=True), (tile, 128))
            return acc + jnp.sum(k_tile * col[tile_rows(i), :][:, :1], axis=0, keepdims=True)

        q = lax.fori_loop(0, tiles, image, jnp.zeros((1, total_ex), jnp.float32))
        square = jnp.sum(prow * q, axis=1, keepdims=True)
        top = jnp.sqrt(jnp.maximum(square, 0.0) + 1e-06)
        if not last:
            row[...] = jnp.broadcast_to(q / top, row.shape)
            col[...] = col_next[...] / top

    center = damping + top
    rho, delta = top / center, damping / center
    zero, one = jnp.zeros_like(center), jnp.ones_like(center)

    def shifted(p):
        low = [delta * v for v in p] + [zero]
        return [a + b for a, b in zip(low, [zero] + list(p))]

    def plus(p, q, factor):
        n = max(len(p), len(q))
        p = list(p) + [zero] * (n - len(p))
        q = list(q) + [zero] * (n - len(q))
        return [a + factor * b for a, b in zip(p, q)]

    sig = one
    direction = [one]
    solution_poly = [one]
    residual = plus([one], shifted(direction), -sig)
    for sweep in range(1, ITERS):
        momentum = 0.5 * (rho * sig) ** 2 if sweep == 1 else (0.5 * rho * sig) ** 2
        sig = 1.0 / (1.0 - momentum / sig)
        direction = plus(residual, direction, momentum)
        solution_poly = plus(solution_poly, direction, sig)
        if sweep + 1 < ITERS:
            residual = plus(residual, shifted(direction), -sig)
    s0, s1, s2, s3 = solution_poly

    inverse = 1.0 / center
    y_ref[...] = full[grp_rows(grp), :] * inverse
    own_cols = pl.ds(pl.multiple_of(grp * group_ex, group_ex), group_ex)
    sc[...] = s0 * y_ref[:, own_cols]
    step_ex = min(256, total_ex)

    def halves(v):
        high = v.astype(jnp.bfloat16)
        return high, (v - high.astype(jnp.float32)).astype(jnp.bfloat16)

    def dot_nt(a, b):
        def product(x, y):
            return lax.dot_general(x, y, NT, preferred_element_type=jnp.float32)

        (a_high, a_low), (b_high, b_low) = halves(a), halves(b)
        return product(a_high, b_high) + (product(a_high, b_low) + product(a_low, b_high))

    def solve(j, c):
        at = pl.ds(pl.multiple_of(j * step_ex, step_ex), step_ex)
        y_tile = y_ref[:, at]
        z_tile = dot_nt(y_ref[...], full[at, :] * inverse)
        sc[...] += dot_nt(y_tile, s1 * y_tile + s2 * z_tile) + dot_nt(z_tile, s3 * z_tile)
        return c

    lax.fori_loop(0, total_ex // step_ex, solve, 0)

    def score_copy(b, slot):
        start = pl.multiple_of(b * examples, examples)
        return pltpu.make_async_remote_copy(
            src_ref=sc.at[pl.ds(start, examples)], dst_ref=sc_land.at[slot],
            send_sem=s_send.at[b], recv_sem=s_recv.at[slot],
            device_id=(grp, b), device_id_type=MESH)

    def score_send(d, c):
        b = lax.rem(blk + d, blocks)
        score_copy(b, blk).start()
        return c

    lax.fori_loop(1, blocks, score_send, 0)
    sc_land[blk] = sc[pl.ds(pl.multiple_of(blk * examples, examples), examples), :]

    def score_arrive(d, c):
        b = lax.rem(blk + d, blocks)
        score_copy(b, b).wait_recv()
        return c

    lax.fori_loop(1, blocks, score_arrive, 0)
    out_ref[...] = jnp.sum(sc_land[...], axis=0)

    def sent(d, c):
        peer, pg, pb = peer_of(d)
        feature_copy(peer, pg, pb, me).wait_send()
        stat_copy(peer, pg, pb, me).wait_send()
        return c

    over_peers(sent)
    for d, h in enumerate(others):
        for q in range(2):
            part_copy(h, d + 1, groups - d - 2, q).wait_send()
            full_copy(h, grp, q).wait_send()
    for h in others:
        prow_copy(h, grp).wait_send()

    def score_sent(d, c):
        score_copy(lax.rem(blk + d, blocks), blk).wait_send()
        return c

    lax.fori_loop(1, blocks, score_sent, 0)


def shards(groups, blocks, activations, out_grads, proj_act, proj_out):
    examples = activations.shape[0] // SEQ
    rank, span = proj_act.shape[1], proj_out.shape[1]
    devices = groups * blocks
    group_ex, total_ex = examples * blocks, examples * devices
    ranks = rank // devices
    width = rank * span // blocks
    act_low = jnp.dot(activations, proj_act, preferred_element_type=jnp.float32).astype(
        jnp.bfloat16
    )
    grad_low = jnp.dot(out_grads, proj_out, preferred_element_type=jnp.float32).astype(jnp.bfloat16)
    vmem = pl.BlockSpec(memory_space=pltpu.VMEM)
    f32 = jnp.float32
    dma = pltpu.SemaphoreType.DMA
    keep = group_ex * ((groups - 1) // 2 + 1) + (0 if groups % 2 else group_ex // 2)
    scores = pl.pallas_call(
        functools.partial(mix_kernel, groups, blocks, examples, ranks, width),
        out_shape=jax.ShapeDtypeStruct((examples, group_ex), f32),
        in_specs=[vmem] * 2,
        out_specs=vmem,
        scratch_shapes=[
            pltpu.VMEM((span // 128, rank * examples, 128), f32),
            pltpu.VMEM((devices, ranks * examples, span), jnp.bfloat16),
            pltpu.VMEM((8, 128), f32),
            pltpu.VMEM((devices, ranks * examples, span), jnp.bfloat16),
            pltpu.VMEM((devices, 8, 128), f32),
            pltpu.VMEM((groups, keep, group_ex), f32),
            pltpu.VMEM((groups - 1, keep, group_ex), f32),
            pltpu.VMEM((groups, keep, group_ex), f32),
            pltpu.VMEM((total_ex, total_ex), f32),
            pltpu.VMEM((8, total_ex), f32),
            pltpu.VMEM((groups, 8, total_ex), f32),
            pltpu.VMEM((8, total_ex), f32),
            pltpu.VMEM((total_ex, 128), f32),
            pltpu.VMEM((total_ex, 128), f32),
            pltpu.VMEM((group_ex, total_ex), f32),
            pltpu.VMEM((group_ex, group_ex), f32),
            pltpu.VMEM((blocks, examples, group_ex), f32),
            dma((devices,)), dma((devices,)), dma((devices,)), dma((devices,)),
            dma((2 * groups,)), dma((2 * groups,)), dma((2 * groups,)), dma((2 * groups,)),
            dma((groups,)), dma((groups,)), dma((blocks,)), dma((blocks,)),
        ],
        compiler_params=pltpu.CompilerParams(
            collective_id=0, has_side_effects=True, vmem_limit_bytes=67043328
        ),
    )(act_low, grad_low)
    return scores * float(examples * groups)


def solution(mesh):
    in_specs = (P(("grp", "blk"), None), P(("grp", "blk"), None), P(), P())
    out_specs = P(("grp", "blk"), None)
    body = functools.partial(shards, mesh.shape["grp"], mesh.shape["blk"])
    return jax.shard_map(body, mesh=mesh, in_specs=in_specs, out_specs=out_specs, check_vma=False)
```

profile of v0, /device:TPU:0, one launch (start us, length us, event | category | flops | bytes accessed | tf_op | source)
XLA Modules:
  0.0 68.7 jit_solution(7299393727477636879)
XLA Ops:
  0.0 0.0 copy-start.1
  0.0 0.0 copy-start
  0.0 5.6 %convolution_convert_fusion.1.act_ref = bf16[1024,128]{1,0:T(8,128)(2,1)} fusion(bf16[1024,3072]{1,0:T(8,128)(2,1)} %param.4, bf16[3072,128]{1,0:T(8,128)(2,1)} %param.6), kind=kOutput, calls=%fused_computation.1 | convolution fusion | flops 805437440 | bytes 7340032 | tf_op jit(solution)/shard_map/dot_general | solution.py:368
  5.6 0.0 copy-done.1
  5.6 0.0 copy-done
  5.6 2.6 %convolution_convert_fusion.grad_ref = bf16[1024,256]{1,0:T(8,128)(2,1)} fusion(bf16[1024,3072]{1,0:T(8,128)(2,1)S(1)} %copy-done, bf16[3072,256]{1,0:T(8,128)(2,1)S(1)} %copy-done.1), kind=kOutput, calls=%fused_computation | convolution fusion | flops 1610874880 | bytes 8388608 | tf_op jit(solution)/shard_map/dot_general | solution.py:371
  8.1 59.3 %shard_map.46 = f32[16,128]{1,0:T(8,128)} custom-call(bf16[1024,128]{1,0:T(8,128)(2,1)} %convolution_convert_fusion.1.act_ref, bf16[1024,256]{1,0:T(8,128)(2,1)} %convolution_convert_fusion.grad_ref), custom_call_target="tpu_custom_call" | custom-call | tf_op jit(solution)/shard_map/pallas_call | solution.py:376
  67.5 1.3 %broadcast_multiply_fusion = f32[16,128]{1,0:T(8,128)} fusion(f32[16,128]{1,0:T(8,128)} %shard_map.46), kind=kLoop, calls=%fused_computation.2 | loop fusion | flops 2048 | bytes 16384 | tf_op jit(solution)/shard_map/mul | solution.py:407
Async XLA Ops:
  0.0 5.6 %copy-start.1 = (bf16[3072,256]{1,0:T(8,128)(2,1)S(1)}, bf16[3072,256]{1,0:T(8,128)(2,1)}, u32[]{:S(2)}) copy-start(bf16[3072,256]{1,0:T(8,128)(2,1)} %param.7) | copy-start | bytes 4718596
  0.0 5.6 %copy-start = (bf16[1024,3072]{1,0:T(8,128)(2,1)S(1)}, bf16[1024,3072]{1,0:T(8,128)(2,1)}, u32[]{:S(2)}) copy-start(bf16[1024,3072]{1,0:T(8,128)(2,1)} %param.5) | copy-start | bytes 18874372
where the time goes:
time: 69 us; the launch traced here: 68.7 us
  Pallas kernels  59.3 us (86%)
  matrix products  8.14 us (12%)
  other arithmetic  1.3 us (2%)
    pallas_call x1, Pallas kernels, shards(): pl.pallas_call(functools.partial(mix_kernel, groups, blocks, examples, ra...  59.3 us
    dot_general x1, matrix products, shards(): jnp.dot(activations, proj_act, preferred_element_type=jnp.float32)  5.57 us
    dot_general x1, matrix products, shards(): jnp.dot(out_grads, proj_out, preferred_element_type=jnp.float32)  2.57 us

commit v1 on v0

v1 whole, which is shorter than its diff:
```python
import functools
import math

import jax
import jax.numpy as jnp
from jax import lax
from jax.experimental import pallas as pl
from jax.experimental.pallas import tpu as pltpu
from jax.sharding import PartitionSpec as P

SEQ = 64
ITERS = 4
damping_rate = 0.5
power_steps = 3
CHUNKS = 2
PARTS = 4
UNITS = 4
MESH = pl.DeviceIdType.MESH
NT = (((1,), (1,)), ((), ()))
TN = (((0,), (0,)), ((), ()))
TILES = [(i, j) for i in range(UNITS) for j in range(i + 1)]


def mix_kernel(
    groups, blocks, examples, ranks, width, slots,
    act_hbm, grad_hbm, pact_hbm, pout_hbm, out_ref,
    act_buf, grad_buf, pact, pout, wide, feat, recv, stat_acc, stat_row, stats_in, plane_row, stats_out,
    part, land1, land2, full, prow_part, prow_land, row, col, col_next, y_ref, pick, sc, sc_land,
    l_sem, w_sem, f_send, f_recv, a_send, a_recv, b_send, b_recv,
    s_send, s_recv, p_send, p_recv, o_send, o_recv,
):
    devices = groups * blocks
    planes = blocks // 2
    near = planes // 2
    cluster = 2 * groups
    group_ex = examples * blocks
    total_ex = group_ex * groups
    unit = total_ex // UNITS
    span = recv.shape[3]
    ex_c = examples // CHUNKS
    grp, blk = lax.axis_index("grp"), lax.axis_index("blk")
    core, plane = lax.rem(blk, 2), lax.div(blk, 2)
    side, row_of = lax.rem(grp, 2), lax.div(grp, 2)
    sign = 1 - 2 * lax.rem(plane, 2)
    solved = core * (groups // 2) + side

    def plane_at(rel):
        return lax.rem(plane + sign * rel + planes, planes)

    def seen_from(source, target):
        flip = 1 - 2 * lax.rem(target, 2)
        return lax.rem((source - target) * flip + planes, planes)

    def peer_of(d):
        rel = lax.rem(near + lax.div(d, cluster), planes)
        j = lax.rem(d, cluster)
        pg = lax.rem(grp + lax.div(j, 2), groups)
        pc = lax.rem(core + lax.rem(j, 2), 2)
        return pg, plane_at(rel), pc

    own = (planes - near) * cluster

    def over_peers(step):
        lax.fori_loop(0, own, step, 0)
        lax.fori_loop(own + 1, devices, step, 0)

    def over_plane(step):
        lax.fori_loop(own + 1, own + cluster, step, 0)

    barrier = pltpu.get_barrier_semaphore()

    def greet(d, c):
        pg, pp, pc = peer_of(d)
        pl.semaphore_signal(barrier, inc=1, device_id=(pg, 2 * pp + pc), device_id_type=MESH)
        return c

    rows_l = act_buf.shape[1]

    def load(k):
        at = pl.ds(k * rows_l, rows_l)
        return (
            pltpu.make_async_copy(act_hbm.at[at], act_buf.at[k % slots], l_sem.at[2 * (k % slots)]),
            pltpu.make_async_copy(grad_hbm.at[at], grad_buf.at[k % slots], l_sem.at[2 * (k % slots) + 1]),
        )

    load_pact = pltpu.make_async_copy(pact_hbm, pact, w_sem.at[0])
    load_pout = pltpu.make_async_copy(pout_hbm, pout, w_sem.at[1])
    load_pact.start()
    load(0)[0].start()
    load_pout.start()
    load(0)[1].start()
    for k in range(1, slots):
        for c in load(k):
            c.start()
    over_peers(greet)
    stat_acc[...] = jnp.zeros_like(stat_acc)

    per_part = rows_l // SEQ
    parts_c = PARTS // CHUNKS

    def project(k):
        first, second = load(k)
        if k == 0:
            load_pact.wait()
        first.wait()
        a_low = jnp.dot(
            act_buf[k % slots], pact[...], preferred_element_type=jnp.float32
        ).astype(jnp.bfloat16)
        if k == 0:
            load_pout.wait()
        second.wait()
        g_low = jnp.dot(
            grad_buf[k % slots], pout[...], preferred_element_type=jnp.float32
        ).astype(jnp.bfloat16)
        if k + slots < PARTS:
            for c in load(k + slots):
                c.start()
        for e in range(per_part):
            here = slice(e * SEQ, (e + 1) * SEQ)
            product = lax.dot_general(
                a_low[here], g_low[here], TN, preferred_element_type=jnp.float32)
            at = (k % parts_c) * per_part + e
            for h in range(wide.shape[0]):
                wide[h, pl.ds(at, a_low.shape[1], stride=ex_c), :] = (
                    product[:, h * 128:(h + 1) * 128])

    def rank_slot(pg, pp, pc):
        return (2 * pp + lax.div(pg, 2)) * groups + 2 * lax.rem(pg, 2) + pc

    def narrow(chunk, slot):
        for r in range(ranks):
            rows = pl.ds(pl.multiple_of((slot * ranks + r) * ex_c, ex_c), ex_c)
            for h in range(wide.shape[0]):
                low = wide[h, rows, :].astype(jnp.bfloat16)
                feat[chunk, slot, r, :, h * 128:(h + 1) * 128] = low
                back = low.astype(jnp.float32)
                stat_acc[...] += jnp.sum(
                    (back * back).reshape(ex_c // 8, 8, 128), axis=0)

    def landing(chunk, pp):
        rel = seen_from(plane, pp)
        u = 2 * lax.div(rel, near) + chunk
        at = (lax.rem(rel, near) * groups + grp) * 2 + core
        return recv.at[u, :, pl.ds(pl.multiple_of(at * ex_c, ex_c), ex_c), :], u

    def feature_copy(chunk, d):
        pg, pp, pc = peer_of(d)
        dst, u = landing(chunk, pp)
        return pltpu.make_async_remote_copy(
            src_ref=feat.at[chunk, rank_slot(pg, pp, pc)], dst_ref=dst,
            send_sem=f_send.at[chunk], recv_sem=f_recv.at[u],
            device_id=(pg, 2 * pp + pc), device_id_type=MESH)

    my_slot = rank_slot(grp, plane, core)

    for chunk in range(CHUNKS):
        for k in range(parts_c):
            project(chunk * parts_c + k)
        if chunk == 0:
            pl.semaphore_wait(barrier, devices - 1)

        def send(d, c, chunk=chunk):
            narrow(chunk, rank_slot(*peer_of(d)))
            feature_copy(chunk, d).start()
            return c

        over_peers(send)
        narrow(chunk, my_slot)
        dst, u = landing(chunk, plane)
        pltpu.make_async_copy(feat.at[chunk, my_slot], dst, f_recv.at[u]).start()

    def stat_in_copy(d):
        pg, pp, pc = peer_of(d)
        return pltpu.make_async_remote_copy(
            src_ref=stat_row, dst_ref=stats_in.at[d - own],
            send_sem=a_send.at[d - own], recv_sem=a_recv.at[d - own],
            device_id=(pg, 2 * pp + pc), device_id_type=MESH)

    def stat_out_copy(rel):
        slot = seen_from(plane, plane_at(rel))
        return pltpu.make_async_remote_copy(
            src_ref=plane_row, dst_ref=stats_out.at[slot],
            send_sem=b_send.at[rel], recv_sem=b_recv.at[slot],
            device_id=(grp, 2 * plane_at(rel) + core), device_id_type=MESH)

    def stat_out_arrive(rel):
        return pltpu.make_async_remote_copy(
            src_ref=plane_row, dst_ref=stats_out.at[rel],
            send_sem=b_send.at[rel], recv_sem=b_recv.at[rel],
            device_id=(grp, 2 * plane_at(rel) + core), device_id_type=MESH)

    stat_row[...] = jnp.sum(stat_acc[...], axis=0, keepdims=True)

    def send_stat(d, c):
        stat_in_copy(d).start()
        return c

    over_plane(send_stat)

    def arrive(u):
        pltpu.make_async_copy(recv.at[u], recv.at[u], f_recv.at[u]).wait()

    def product(u, v):
        total = None
        for r in range(ranks):
            term = lax.dot_general(
                recv[u, r], recv[v, r], NT, preferred_element_type=jnp.float32)
            total = term if total is None else total + term
        return total

    ones = jnp.ones((8, span), jnp.bfloat16)
    scale = 1.0 / math.sqrt(width)

    def sums(u):
        total = None
        for r in range(ranks):
            term = lax.dot_general(ones, recv[u, r], NT, preferred_element_type=jnp.float32)
            total = term if total is None else total + term
        prow_part[:, u * unit:(u + 1) * unit] = total[:1] * scale

    partner = (grp, blk + 1 - 2 * core)
    across = (grp + 1 - 2 * side, blk)

    def spot(i):
        (i0, j0), (i1, j1) = TILES[2 * i], TILES[2 * i + 1]
        return i0 + core * (i1 - i0), j0 + core * (j1 - j0)

    def spot_ref(i):
        at, to = spot(i)
        return full.at[pl.ds(pl.multiple_of(at * unit, unit), unit),
                       pl.ds(pl.multiple_of(to * unit, unit), unit)]

    def give(i):
        return pltpu.make_async_remote_copy(
            src_ref=part.at[2 * i + 1 - core], dst_ref=land1.at[i],
            send_sem=s_send.at[3 * i], recv_sem=s_recv.at[3 * i],
            device_id=partner, device_id_type=MESH)

    def swap(i):
        return pltpu.make_async_remote_copy(
            src_ref=part.at[2 * i + core], dst_ref=land2.at[i],
            send_sem=s_send.at[3 * i + 1], recv_sem=s_recv.at[3 * i + 1],
            device_id=across, device_id_type=MESH)

    def share(i):
        return pltpu.make_async_remote_copy(
            src_ref=spot_ref(i), dst_ref=spot_ref(i),
            send_sem=s_send.at[3 * i + 2], recv_sem=s_recv.at[3 * i + 2],
            device_id=partner, device_id_type=MESH)

    def second(i):
        give(i).wait_recv()
        mine = 2 * i + core
        part[mine] = part[mine] + land1[i]
        swap(i).start()

    def third(i):
        swap(i).wait_recv()
        at, to = spot(i)
        full[pl.ds(pl.multiple_of(at * unit, unit), unit),
             pl.ds(pl.multiple_of(to * unit, unit), unit)] = part[2 * i + core] + land2[i]
        share(i).start()

    def mirror(t):
        at, to = TILES[t]
        if at != to:
            a, b = slice(at * unit, (at + 1) * unit), slice(to * unit, (to + 1) * unit)
            full[b, a] = full[a, b].T

    def prow_copy(m):
        pg = grp + (1 - 2 * side) * (m % 2)
        pb = blk + (1 - 2 * core) * (m // 2)
        return pltpu.make_async_remote_copy(
            src_ref=prow_part, dst_ref=prow_land.at[m - 1],
            send_sem=p_send.at[m - 1], recv_sem=p_recv.at[m - 1],
            device_id=(pg, pb), device_id_type=MESH)

    last = UNITS - 1
    pairs = len(TILES) // 2
    early = [i for i in range(pairs) if TILES[2 * i + 1][0] < last]
    late = [i for i in range(pairs) if TILES[2 * i][0] == last]
    sent = 0
    for u in range(last):
        arrive(u)
        sums(u)
        for v in range(u + 1):
            part[u * (u + 1) // 2 + v] = product(u, v)
        if u == 0:
            def arrive_stat(d, c):
                stat_in_copy(d).wait_recv()
                return c

            over_plane(arrive_stat)
            stats_in[0] = stat_row[...]
            plane_row[...] = jnp.sum(stats_in[...], axis=0)
            for rel in range(1, planes):
                stat_out_copy(rel).start()
            stats_out[0] = plane_row[...]
        while sent < len(early) and 2 * sent + 1 < (u + 1) * (u + 2) // 2:
            give(sent).start()
            sent += 1
        if u == last - 1:
            for i in early:
                second(i)
            for i in early:
                third(i)
    arrive(last)
    base = last * (last + 1) // 2
    for n, i in enumerate(late):
        v = 2 * n + 1 - core
        part[base + v] = product(last, v)
        give(i).start()
    sums(last)
    for m in range(1, 4):
        prow_copy(m).start()
    for n, i in enumerate(late):
        v = 2 * n + core
        part[base + v] = product(last, v)
        second(i)
    for i in early:
        share(i).wait_recv()
    for t in range(base):
        mirror(t)
    for rel in range(1, planes):
        stat_out_arrive(rel).wait_recv()
    total = jnp.sum(jnp.sum(stats_out[...], axis=0), axis=1, keepdims=True)
    damping = damping_rate * total / (width * blocks)

    def rel_row(q, pc, ch):
        rel = seen_from(q, plane)
        u = 2 * lax.div(rel, near) + ch
        return u * unit + ((lax.rem(rel, near) * groups + solved) * 2 + pc) * ex_c

    pieces = [(q, pc, ch) for q in range(planes) for pc in range(2) for ch in range(CHUNKS)]
    lane = lax.broadcasted_iota(jnp.int32, (2 * ex_c, total_ex), 1)
    sub = lax.broadcasted_iota(jnp.int32, (2 * ex_c, total_ex), 0)
    for n in range(0, len(pieces), 2):
        a, b = rel_row(*pieces[n]), rel_row(*pieces[n + 1])
        at = jnp.where(sub < ex_c, a + sub, b + sub - ex_c)
        pick[n * ex_c:(n + 2) * ex_c, :] = jnp.where(at == lane, 1.0, 0.0).astype(jnp.bfloat16)

    for m in range(1, 4):
        prow_copy(m).wait_recv()
    row[...] = jnp.broadcast_to(prow_part[...] + jnp.sum(prow_land[...], axis=0), row.shape)
    for i in late:
        third(i)
    for i in late:
        share(i).wait_recv()
    for t in range(base, len(TILES)):
        mirror(t)

    tile = 128
    tiles = total_ex // tile

    def tile_rows(i):
        return pl.ds(pl.multiple_of(i * tile, tile), tile)

    def turn(i, c):
        spots = lax.broadcasted_iota(jnp.int32, (tile, total_ex), 0) + i * tile
        lanes = lax.broadcasted_iota(jnp.int32, (tile, total_ex), 1)
        picked = jnp.where(spots == lanes, row[:1, :], 0.0)
        col[tile_rows(i), :] = jnp.broadcast_to(
            jnp.sum(picked, axis=1, keepdims=True), (tile, 128))
        return c

    lax.fori_loop(0, tiles, turn, 0)
    top = None
    for step in range(power_steps):
        final = step + 1 == power_steps
        prow = row[:1, :]

        def image(i, acc):
            k_tile = full[tile_rows(i), :]
            if not final:
                col_next[tile_rows(i), :] = jnp.broadcast_to(
                    jnp.sum(k_tile * prow, axis=1, keepdims=True), (tile, 128))
            return acc + jnp.sum(k_tile * col[tile_rows(i), :][:, :1], axis=0, keepdims=True)

        q = lax.fori_loop(0, tiles, image, jnp.zeros((1, total_ex), jnp.float32))
        square = jnp.sum(prow * q, axis=1, keepdims=True)
        top = jnp.sqrt(jnp.maximum(square, 0.0) + 1e-06)
        if not final:
            row[...] = jnp.broadcast_to(q / top, row.shape)
            col[...] = col_next[...] / top

    center = damping + top
    rho, delta = top / center, damping / center
    zero, one = jnp.zeros_like(center), jnp.ones_like(center)

    def shifted(p):
        low = [delta * v for v in p] + [zero]
        return [a + b for a, b in zip(low, [zero] + list(p))]

    def plus(p, q, factor):
        n = max(len(p), len(q))
        p = list(p) + [zero] * (n - len(p))
        q = list(q) + [zero] * (n - len(q))
        return [a + factor * b for a, b in zip(p, q)]

    sig = one
    direction = [one]
    solution_poly = [one]
    residual = plus([one], shifted(direction), -sig)
    for sweep in range(1, ITERS):
        momentum = 0.5 * (rho * sig) ** 2 if sweep == 1 else (0.5 * rho * sig) ** 2
        sig = 1.0 / (1.0 - momentum / sig)
        direction = plus(residual, direction, momentum)
        solution_poly = plus(solution_poly, direction, sig)
        if sweep + 1 < ITERS:
            residual = plus(residual, shifted(direction), -sig)
    s0, s1, s2, s3 = solution_poly

    inverse = 1.0 / center
    for n, piece in enumerate(pieces):
        y_ref[n * ex_c:(n + 1) * ex_c, :] = (
            full[pl.ds(pl.multiple_of(rel_row(*piece), ex_c), ex_c), :] * inverse)
    step_ex = min(256, total_ex)

    def halves(v):
        high = v.astype(jnp.bfloat16)
        return high, (v - high.astype(jnp.float32)).astype(jnp.bfloat16)

    def nt(x, y):
        return lax.dot_general(x, y, NT, preferred_element_type=jnp.float32)

    def dot_nt(a, b):
        (a_high, a_low), (b_high, b_low) = halves(a), halves(b)
        return nt(a_high, b_high) + (nt(a_high, b_low) + nt(a_low, b_high))

    sc[...] = jnp.zeros_like(sc)

    def solve(j, c):
        at = pl.ds(pl.multiple_of(j * step_ex, step_ex), step_ex)
        y_tile = y_ref[:, at]
        z_tile = dot_nt(y_ref[...], full[at, :] * inverse)
        y_high, y_low = halves(y_tile)
        sc[...] += (s0 * (nt(y_high, pick[:, at]) + nt(y_low, pick[:, at]))
                    + dot_nt(y_tile, s1 * y_tile + s2 * z_tile) + dot_nt(z_tile, s3 * z_tile))
        return c

    lax.fori_loop(0, total_ex // step_ex, solve, 0)

    block = 2 * plane + row_of

    def score_copy(b):
        start = pl.multiple_of(b * examples, examples)
        return pltpu.make_async_remote_copy(
            src_ref=sc.at[pl.ds(start, examples)], dst_ref=sc_land.at[block],
            send_sem=o_send.at[b], recv_sem=o_recv.at[block],
            device_id=(solved, b), device_id_type=MESH)

    def score_self():
        start = pl.multiple_of(blk * examples, examples)
        return pltpu.make_async_copy(
            sc.at[pl.ds(start, examples)], sc_land.at[block], o_recv.at[block])

    def score_send(d, c):
        score_copy(lax.rem(blk + d, blocks)).start()
        return c

    lax.fori_loop(1, blocks, score_send, 0)

    @pl.when(solved == grp)
    def _():
        score_self().start()

    @pl.when(solved != grp)
    def _():
        score_copy(blk).start()

    def score_arrive(k, c):
        pltpu.make_async_copy(sc_land.at[k], sc_land.at[k], o_recv.at[k]).wait()
        return c

    lax.fori_loop(0, blocks, score_arrive, 0)
    out_ref[...] = jnp.sum(sc_land[...], axis=0)

    for chunk in range(CHUNKS):
        whole = feat.at[chunk, pl.ds(0, devices - 1)]
        pltpu.make_async_copy(whole, whole, f_send.at[chunk]).wait()

    def stat_gone(d, c):
        stat_in_copy(d).wait_send()
        return c

    over_plane(stat_gone)
    for rel in range(1, planes):
        stat_out_copy(rel).wait_send()
    for i in range(pairs):
        give(i).wait_send()
        swap(i).wait_send()
        share(i).wait_send()
    for m in range(1, 4):
        prow_copy(m).wait_send()

    def score_gone(d, c):
        score_copy(lax.rem(blk + d, blocks)).wait_send()
        return c

    lax.fori_loop(1, blocks, score_gone, 0)

    @pl.when(solved != grp)
    def _():
        score_copy(blk).wait_send()


def shards(groups, blocks, activations, out_grads, proj_act, proj_out):
    tokens, depth = activations.shape
    examples = tokens // SEQ
    rank, span = proj_act.shape[1], proj_out.shape[1]
    devices = groups * blocks
    group_ex, total_ex = examples * blocks, examples * devices
    ranks = rank // devices
    width = rank * span // blocks
    planes, unit = blocks // 2, total_ex // UNITS
    ex_c, rows_l = examples // CHUNKS, tokens // PARTS
    slots = PARTS if total_ex <= 1024 else PARTS // 2
    vmem = pl.BlockSpec(memory_space=pltpu.VMEM)
    hbm = pl.BlockSpec(memory_space=pl.ANY)
    f32, low = jnp.float32, jnp.bfloat16
    dma = pltpu.SemaphoreType.DMA
    tiles = len(TILES)
    scores = pl.pallas_call(
        functools.partial(mix_kernel, groups, blocks, examples, ranks, width, slots),
        out_shape=jax.ShapeDtypeStruct((examples, group_ex), f32),
        in_specs=[hbm] * 4,
        out_specs=vmem,
        scratch_shapes=[
            pltpu.VMEM((slots, rows_l, depth), low),
            pltpu.VMEM((slots, rows_l, depth), low),
            pltpu.VMEM((depth, rank), low),
            pltpu.VMEM((depth, span), low),
            pltpu.VMEM((span // 128, rank * ex_c, 128), f32),
            pltpu.VMEM((CHUNKS, devices, ranks, ex_c, span), low),
            pltpu.VMEM((UNITS, ranks, unit, span), low),
            pltpu.VMEM((8, 128), f32),
            pltpu.VMEM((1, 128), f32),
            pltpu.VMEM((2 * groups, 1, 128), f32),
            pltpu.VMEM((1, 128), f32),
            pltpu.VMEM((planes, 1, 128), f32),
            pltpu.VMEM((tiles, unit, unit), f32),
            pltpu.VMEM((tiles // 2, unit, unit), f32),
            pltpu.VMEM((tiles // 2, unit, unit), f32),
            pltpu.VMEM((total_ex, total_ex), f32),
            pltpu.VMEM((1, total_ex), f32),
            pltpu.VMEM((3, 1, total_ex), f32),
            pltpu.VMEM((8, total_ex), f32),
            pltpu.VMEM((total_ex, 128), f32),
            pltpu.VMEM((total_ex, 128), f32),
            pltpu.VMEM((group_ex, total_ex), f32),
            pltpu.VMEM((group_ex, total_ex), low),
            pltpu.VMEM((group_ex, group_ex), f32),
            pltpu.VMEM((blocks, examples, group_ex), f32),
            dma((2 * slots,)), dma((2,)), dma((CHUNKS,)), dma((UNITS,)),
            dma((2 * groups,)), dma((2 * groups,)), dma((planes,)), dma((planes,)),
            dma((3 * tiles // 2,)), dma((3 * tiles // 2,)), dma((3,)), dma((3,)),
            dma((blocks,)), dma((blocks,)),
        ],
        compiler_params=pltpu.CompilerParams(
            collective_id=0, has_side_effects=True, vmem_limit_bytes=67043328
        ),
    )(activations, out_grads, proj_act, proj_out)
    return scores * float(examples * groups)


def solution(mesh):
    in_specs = (P(("grp", "blk"), None), P(("grp", "blk"), None), P(), P())
    out_specs = P(("grp", "blk"), None)
    body = functools.partial(shards, mesh.shape["grp"], mesh.shape["blk"])
    return jax.shard_map(body, mesh=mesh, in_specs=in_specs, out_specs=out_specs, check_vma=False)
```

time: 69 us -> 57.3 us (0.83)
  matrix products: 8.14 us -> 0 us
  Pallas kernels: 59.3 us -> 55.8 us
    dot_general x2 -> x0, matrix products: 8.14 us -> none  [the longest x1 5.57 us: shards(): jnp.dot(activations, proj_act, preferred_element_type=jnp.float32)]
    pallas_call x1, Pallas kernels: 59.3 us -> 55.8 us  [shards(): pl.pallas_call(functools.partial(mix_kernel, groups, blocks, examples, ra...]
where the time goes in v1:
time: 57.3 us; the launch traced here: 57.1 us
  Pallas kernels  55.8 us (97%)
  other arithmetic  1.3 us (2%)
    pallas_call x1, Pallas kernels, shards(): pl.pallas_call(functools.partial(mix_kernel, groups, blocks, examples, ra...  55.8 us
    mul x1, other arithmetic, shards(): return scores * float(examples * groups)  1.3 us

profile of v1, /device:TPU:0, one launch (start us, length us, event | category | flops | bytes accessed | tf_op | source)
XLA Modules:
  0.0 57.1 jit_solution(14039591892713817883)
XLA Ops:
  0.0 55.8 %shard_map.46 = f32[16,128]{1,0:T(8,128)} custom-call(bf16[1024,3072]{1,0:T(8,128)(2,1)} %act_hbm.1, bf16[1024,3072]{1,0:T(8,128)(2,1)} %grad_hbm.1, bf16[3072,128]{1,0:T(8,128)(2,1)} %pact_hbm.1, bf16[3072,256]{1,0:T(8,128)(2,1)} %pout_hbm.1), custom_call_target="tpu_custom_call" | custom-call | tf_op jit(solution)/shard_map/pallas_call | solution.py:523
  55.8 1.3 %broadcast_multiply_fusion = f32[16,128]{1,0:T(8,128)} fusion(f32[16,128]{1,0:T(8,128)} %shard_map.46), kind=kLoop, calls=%fused_computation | loop fusion | flops 2048 | bytes 16384 | tf_op jit(solution)/shard_map/mul | solution.py:563

commit v2 on v1

v2 whole, which is shorter than its diff:
```python
import functools
import math

import jax
import jax.numpy as jnp
from jax import lax
from jax.experimental import pallas as pl
from jax.experimental.pallas import tpu as pltpu
from jax.sharding import PartitionSpec as P

SEQ = 64
ITERS = 4
damping_rate = 0.5
power_steps = 3
CHUNKS = 2
PARTS = 4
AHEAD = 2
UNITS = 4
MESH = pl.DeviceIdType.MESH
NT = (((1,), (1,)), ((), ()))
TN = (((0,), (0,)), ((), ()))
TILES = [(i, j) for i in range(UNITS) for j in range(i + 1)]


def mix_kernel(
    groups, blocks, examples, ranks, width, slots, batch, keep,
    act_hbm, grad_hbm, pact_hbm, pout_hbm, out_ref,
    act_buf, grad_buf, pact, pout, wide, feat, recv, stat_acc, stat_row, stats,
    land, full, w_high, w_low, prow_part, prow_land, row, col, y_high, y_low, pick, acc, sc, sc_land,
    l_sem, w_sem, f_send, f_recv, t_send, t_recv, k_send, k_recv, p_send, p_recv, o_send, o_recv,
):
    devices = groups * blocks
    planes = blocks // 2
    near = planes // 2
    targets = 2 * blocks
    group_ex = examples * blocks
    total_ex = group_ex * groups
    unit = total_ex // UNITS
    span = recv.shape[3]
    ex_c = examples // CHUNKS
    core_groups = groups // 2
    grp, blk = lax.axis_index("grp"), lax.axis_index("blk")
    me = grp * blocks + blk
    core, plane = lax.rem(blk, 2), lax.div(blk, 2)
    sign = 1 - 2 * lax.rem(plane, 2)
    far_end = groups - 1
    is_owner = lax.rem(grp, far_end) == 0
    block = 2 * plane + lax.div(grp, far_end)

    def plane_at(rel):
        return lax.rem(plane + sign * rel + planes, planes)

    def seen_from(source, target):
        flip = 1 - 2 * lax.rem(target, 2)
        return lax.rem((source - target) * flip + planes, planes)

    def target_of(d):
        rel = lax.rem(near + lax.div(d, 4), planes)
        j = lax.rem(d, 4)
        side = lax.rem(grp + lax.div(j, 2), 2)
        pc = lax.rem(core + lax.rem(j, 2), 2)
        return side, plane_at(rel), pc

    barrier = pltpu.get_barrier_semaphore()

    def greet(d, c):
        peer = lax.rem(me + d, devices)
        pl.semaphore_signal(
            barrier, inc=1, device_id=(lax.div(peer, blocks), lax.rem(peer, blocks)),
            device_id_type=MESH)
        return c

    rows_l = act_buf.shape[1]

    def load(k):
        at = pl.ds(k * rows_l, rows_l)
        return (
            pltpu.make_async_copy(act_hbm.at[at], act_buf.at[k % slots], l_sem.at[2 * (k % slots)]),
            pltpu.make_async_copy(grad_hbm.at[at], grad_buf.at[k % slots], l_sem.at[2 * (k % slots) + 1]),
        )

    load_pact = pltpu.make_async_copy(pact_hbm, pact, w_sem.at[0])
    load_pout = pltpu.make_async_copy(pout_hbm, pout, w_sem.at[1])
    load_pact.start()
    load_pout.start()
    for k in range(AHEAD):
        for c in load(k):
            c.start()
    lax.fori_loop(1, devices, greet, 0)
    stat_acc[...] = jnp.zeros_like(stat_acc)

    per_part = rows_l // SEQ
    parts_c = PARTS // CHUNKS

    def project(k):
        loads = load(k)
        if k == 0:
            load_pact.wait()
            load_pout.wait()
        for c in loads:
            c.wait()
        if k + AHEAD < PARTS and AHEAD < slots:
            for c in load(k + AHEAD):
                c.start()
        a_low = jnp.dot(
            act_buf[k % slots], pact[...], preferred_element_type=jnp.float32
        ).astype(jnp.bfloat16)
        g_low = jnp.dot(
            grad_buf[k % slots], pout[...], preferred_element_type=jnp.float32
        ).astype(jnp.bfloat16)
        if k + AHEAD < PARTS and AHEAD == slots:
            for c in load(k + AHEAD):
                c.start()
        for e in range(per_part):
            here = slice(e * SEQ, (e + 1) * SEQ)
            product = lax.dot_general(
                a_low[here], g_low[here], TN, preferred_element_type=jnp.float32)
            at = (k % parts_c) * per_part + e
            for h in range(wide.shape[0]):
                wide[h, pl.ds(at, a_low.shape[1], stride=ex_c), :] = (
                    product[:, h * 128:(h + 1) * 128])

    def narrow(chunk, slot):
        for r in range(ranks):
            rows = pl.ds(pl.multiple_of((slot * ranks + r) * ex_c, ex_c), ex_c)
            for h in range(wide.shape[0]):
                low = wide[h, rows, :].astype(jnp.bfloat16)
                feat[chunk, slot, r, :, h * 128:(h + 1) * 128] = low
                back = low.astype(jnp.float32)
                stat_acc[...] += jnp.sum((back * back).reshape(ex_c // 8, 8, 128), axis=0)

    def landing(chunk, pp):
        rel = seen_from(plane, pp)
        u = 2 * lax.div(rel, near) + chunk
        at = (lax.rem(rel, near) * groups + grp) * 2 + core
        return recv.at[u, :, pl.ds(pl.multiple_of(at * ex_c, ex_c), ex_c), :], u

    def either(side, pp, pc, local, remote):
        mine = jnp.logical_and(side * far_end == grp, 2 * pp + pc == blk)
        pl.when(mine)(local)
        pl.when(jnp.logical_not(mine))(remote)

    for chunk in range(CHUNKS):
        for k in range(parts_c):
            project(chunk * parts_c + k)
        if chunk == 0:
            pl.semaphore_wait(barrier, devices - 1)

        def send(d, c, chunk=chunk):
            side, pp, pc = target_of(d)
            slot = (2 * pp + side) * 2 + pc
            narrow(chunk, slot)
            dst, u = landing(chunk, pp)

            def local():
                pltpu.make_async_copy(feat.at[chunk, slot], dst, f_recv.at[u]).start()

            def remote():
                pltpu.make_async_remote_copy(
                    src_ref=feat.at[chunk, slot], dst_ref=dst,
                    send_sem=f_send.at[chunk], recv_sem=f_recv.at[u],
                    device_id=(side * far_end, 2 * pp + pc), device_id_type=MESH).start()

            either(side, pp, pc, local, remote)
            return c

        lax.fori_loop(0, targets, send, 0)

    stat_row[...] = jnp.sum(stat_acc[...], axis=0, keepdims=True)

    def send_stat(d, c):
        side, pp, pc = target_of(d)

        def local():
            pltpu.make_async_copy(stat_row, stats.at[me], t_recv).start()

        def remote():
            pltpu.make_async_remote_copy(
                src_ref=stat_row, dst_ref=stats.at[me], send_sem=t_send, recv_sem=t_recv,
                device_id=(side * far_end, 2 * pp + pc), device_id_type=MESH).start()

        either(side, pp, pc, local, remote)
        return c

    lax.fori_loop(0, targets, send_stat, 0)

    ones = jnp.ones((8, span), jnp.bfloat16)
    norm = 1.0 / math.sqrt(width)
    partner = (grp, blk + 1 - 2 * core)
    pieces = [(q, pc, ch) for q in range(planes) for pc in range(2) for ch in range(CHUNKS)]

    def nt(x, y):
        return lax.dot_general(x, y, NT, preferred_element_type=jnp.float32)

    def halves(v):
        high = v.astype(jnp.bfloat16)
        return high, (v - high.astype(jnp.float32)).astype(jnp.bfloat16)

    def arrive(u):
        pltpu.make_async_copy(recv.at[u], recv.at[u], f_recv.at[u]).wait()

    def over_ranks(left, v):
        total = None
        for r in range(ranks):
            term = nt(left(r), recv[v, r])
            total = term if total is None else total + term
        return total

    def area(u, v):
        return slice(u * unit, (u + 1) * unit), slice(v * unit, (v + 1) * unit)

    def tile_copy(u, v):
        t = u * (u + 1) // 2 + v
        a, b = area(u, v)
        return pltpu.make_async_remote_copy(
            src_ref=full.at[a, b], dst_ref=land.at[t],
            send_sem=k_send.at[t], recv_sem=k_recv.at[t],
            device_id=partner, device_id_type=MESH)

    def prow_copy():
        return pltpu.make_async_remote_copy(
            src_ref=prow_part, dst_ref=prow_land, send_sem=p_send, recv_sem=p_recv,
            device_id=partner, device_id_type=MESH)

    def rel_row(group, q, pc, ch):
        rel = seen_from(q, plane)
        u = 2 * lax.div(rel, near) + ch
        return u * unit + ((lax.rem(rel, near) * groups + group) * 2 + pc) * ex_c

    def own_work():
        for u in range(UNITS):
            arrive(u)
            if u == 0:
                pltpu.make_async_copy(stats, stats, t_recv).wait()
            total = jnp.sum(jnp.sum(stats[...], axis=0), axis=1, keepdims=True)
            shrink = 1.0 / (total + 1e-30)
            for v in range(u + 1):
                a, b = area(u, v)
                full[a, b] = over_ranks(lambda r, u=u: recv[u, r], v)
                tile_copy(u, v).start()
            prow_part[:, u * unit:(u + 1) * unit] = over_ranks(lambda r: ones, u)[:1] * norm
            if u == UNITS - 1:
                prow_copy().start()
            for v in range(u + 1):
                t = u * (u + 1) // 2 + v
                a, b = area(u, v)
                tile_copy(u, v).wait_recv()
                tile_copy(u, v).wait_send()
                both = full[a, b] + land[t]
                full[a, b] = both
                if keep:
                    w_high[a, b], w_low[a, b] = halves(both * shrink)
                if u != v:
                    both = both.T
                    full[b, a] = both
                    if keep:
                        w_high[b, a], w_low[b, a] = halves(both * shrink)
        damping = damping_rate * total / (width * blocks)
        prow_copy().wait_recv()
        prow_copy().wait_send()

        row[...] = jnp.broadcast_to(prow_part[...] + prow_land[...], row.shape)

        def upright(values):
            for c in range(total_ex // 128):
                here = slice(c * 128, (c + 1) * 128)
                col[here, :] = jnp.broadcast_to(values[:, here], (128, 128)).T

        def image():
            def block_sum(i, total):
                for e in range(16):
                    rows = pl.ds(i * 128 + e * 8, 8)
                    weight = jnp.concatenate([col[rows, :]] * (total_ex // 128), axis=1)
                    total = total + full[rows, :] * weight
                return total

            start = jnp.zeros((8, total_ex), jnp.float32)
            if total_ex <= 512:
                for i in range(total_ex // 128):
                    start = block_sum(i, start)
            else:
                start = lax.fori_loop(
                    0, total_ex // 128,
                    lambda i, t: block_sum(i, t), start)
            return jnp.sum(start, axis=0, keepdims=True)

        step_ex = min(256, total_ex)

        def prepare(first):
            for n in range(batch):
                group = core * core_groups + first + n
                for m in range(0, len(pieces), 2):
                    at, to = rel_row(group, *pieces[m]), rel_row(group, *pieces[m + 1])
                    at, to = pl.multiple_of(at, ex_c), pl.multiple_of(to, ex_c)
                    y = jnp.concatenate(
                        [full[pl.ds(at, ex_c), :], full[pl.ds(to, ex_c), :]], axis=0) * shrink
                    here = slice(n * group_ex + m * ex_c, n * group_ex + (m + 2) * ex_c)
                    y_high[here, :], y_low[here, :] = halves(y)
                    lane = lax.broadcasted_iota(jnp.int32, (2 * ex_c, total_ex), 1)
                    sub = lax.broadcasted_iota(jnp.int32, (2 * ex_c, total_ex), 0)
                    spot = jnp.where(sub < ex_c, at + sub, to + sub - ex_c)
                    pick[here, :] = jnp.where(spot == lane, 1.0, 0.0).astype(jnp.bfloat16)

        def powers(at, fresh):
            yh, yl = y_high[...], y_low[...]
            if keep:
                wh, wl = w_high[at, :], w_low[at, :]
            else:
                wh, wl = halves(full[at, :] * shrink)
            vh, vl = halves(nt(yh, wh) + (nt(yh, wl) + nt(yl, wh)))
            for n in range(batch):
                here = slice(n * group_ex, (n + 1) * group_ex)
                ah, al, ph = y_high[here, at], y_low[here, at], pick[here, at]
                bh, bl = vh[here], vl[here]
                right = jnp.concatenate([ah, ph], axis=0)
                one = nt(ah, right) + nt(al, right)
                one_low = nt(ah, al)
                both_h = jnp.concatenate([ah, bh], axis=0)
                both_l = jnp.concatenate([al, bl], axis=0)
                two = nt(bh, both_h) + (nt(bh, both_l) + nt(bl, both_h))
                terms = (one[:, group_ex:], one[:, :group_ex] + one_low,
                         two[:, :group_ex], two[:, group_ex:])
                for k, term in enumerate(terms):
                    acc[n, k] = term if fresh else acc[n, k] + term

        def multiply():
            if total_ex <= 512:
                for k in range(total_ex // step_ex):
                    powers(slice(k * step_ex, (k + 1) * step_ex), k == 0)
            else:
                acc[...] = jnp.zeros_like(acc)

                def one_step(k, c):
                    powers(pl.ds(pl.multiple_of(k * step_ex, step_ex), step_ex), False)
                    return c

                lax.fori_loop(0, total_ex // step_ex, one_step, 0)

        prepare(0)
        multiply()
        values = row[:1, :]
        top = None
        for step in range(power_steps):
            upright(values)
            q = image()
            square = jnp.sum(values * q, axis=1, keepdims=True)
            top = jnp.sqrt(jnp.maximum(square, 0.0) + 1e-06)
            values = q / top

        center = damping + top
        rho, delta = top / center, damping / center
        zero, one = jnp.zeros_like(center), jnp.ones_like(center)

        def shifted(p):
            low = [delta * v for v in p] + [zero]
            return [a + b for a, b in zip(low, [zero] + list(p))]

        def plus(p, q, factor):
            n = max(len(p), len(q))
            p = list(p) + [zero] * (n - len(p))
            q = list(q) + [zero] * (n - len(q))
            return [a + factor * b for a, b in zip(p, q)]

        sig = one
        direction = [one]
        solution_poly = [one]
        residual = plus([one], shifted(direction), -sig)
        for sweep in range(1, ITERS):
            momentum = 0.5 * (rho * sig) ** 2 if sweep == 1 else (0.5 * rho * sig) ** 2
            sig = 1.0 / (1.0 - momentum / sig)
            direction = plus(residual, direction, momentum)
            solution_poly = plus(solution_poly, direction, sig)
            if sweep + 1 < ITERS:
                residual = plus(residual, shifted(direction), -sig)
        stretch = (total + 1e-30) / center
        factors = []
        power = stretch
        for coefficient in solution_poly:
            factors.append(coefficient * power)
            power = power * stretch

        for first in range(0, core_groups, batch):
            if first:
                prepare(first)
                multiply()
            for n in range(batch):
                score = factors[0] * acc[n, 0]
                for k in range(1, ITERS):
                    score = score + factors[k] * acc[n, k]
                sc[first + n] = score

                def send_score(d, c, n=first + n):
                    b = lax.rem(blk + blocks // 2 + d, blocks)
                    group = core * core_groups + n
                    src = sc.at[n, pl.ds(pl.multiple_of(b * examples, examples), examples)]
                    mine = jnp.logical_and(group == grp, b == blk)

                    @pl.when(mine)
                    def _():
                        pltpu.make_async_copy(src, sc_land.at[block], o_recv.at[block]).start()

                    @pl.when(jnp.logical_not(mine))
                    def _():
                        pltpu.make_async_remote_copy(
                            src_ref=src, dst_ref=sc_land.at[block],
                            send_sem=o_send.at[n * blocks + b], recv_sem=o_recv.at[block],
                            device_id=(group, b), device_id_type=MESH).start()

                    return c

                lax.fori_loop(0, blocks, send_score, 0)

    pl.when(is_owner)(own_work)

    def score_arrive(k, c):
        pltpu.make_async_copy(sc_land.at[k], sc_land.at[k], o_recv.at[k]).wait()
        return c

    lax.fori_loop(0, blocks, score_arrive, 0)
    out_ref[...] = jnp.sum(sc_land[...], axis=0)

    def gone(count):
        for chunk in range(CHUNKS):
            sent = feat.at[chunk, pl.ds(0, count)]
            pltpu.make_async_copy(sent, sent, f_send.at[chunk]).wait()
        rows = stats.at[pl.ds(0, count)]
        pltpu.make_async_copy(rows, rows, t_send).wait()

    @pl.when(is_owner)
    def _():
        gone(targets - 1)
        for n in range(core_groups):
            def score_gone(d, c, n=n):
                b = lax.rem(blk + d, blocks)
                group = core * core_groups + n
                src = sc.at[n, pl.ds(pl.multiple_of(b * examples, examples), examples)]

                @pl.when(jnp.logical_not(jnp.logical_and(group == grp, b == blk)))
                def _():
                    pltpu.make_async_copy(src, src, o_send.at[n * blocks + b]).wait()

                return c

            lax.fori_loop(0, blocks, score_gone, 0)

    @pl.when(jnp.logical_not(is_owner))
    def _():
        gone(targets)


def shards(groups, blocks, activations, out_grads, proj_act, proj_out):
    tokens, depth = activations.shape
    examples = tokens // SEQ
    rank, span = proj_act.shape[1], proj_out.shape[1]
    devices, targets = groups * blocks, 2 * blocks
    group_ex, total_ex = examples * blocks, examples * devices
    ranks = rank // targets
    width = rank * span // blocks
    unit = total_ex // UNITS
    ex_c, rows_l = examples // CHUNKS, tokens // PARTS
    small = total_ex <= 1024
    slots = PARTS if small else AHEAD
    batch = groups // 2 if small else 1
    split = total_ex if small else 8
    vmem = pl.BlockSpec(memory_space=pltpu.VMEM)
    hbm = pl.BlockSpec(memory_space=pl.ANY)
    f32, low = jnp.float32, jnp.bfloat16
    dma = pltpu.SemaphoreType.DMA
    tiles = len(TILES)
    scores = pl.pallas_call(
        functools.partial(mix_kernel, groups, blocks, examples, ranks, width, slots, batch, small),
        out_shape=jax.ShapeDtypeStruct((examples, group_ex), f32),
        in_specs=[hbm] * 4,
        out_specs=vmem,
        scratch_shapes=[
            pltpu.VMEM((slots, rows_l, depth), low),
            pltpu.VMEM((slots, rows_l, depth), low),
            pltpu.VMEM((depth, rank), low),
            pltpu.VMEM((depth, span), low),
            pltpu.VMEM((span // 128, rank * ex_c, 128), f32),
            pltpu.VMEM((CHUNKS, targets, ranks, ex_c, span), low),
            pltpu.VMEM((UNITS, ranks, unit, span), low),
            pltpu.VMEM((8, 128), f32),
            pltpu.VMEM((1, 128), f32),
            pltpu.VMEM((devices, 1, 128), f32),
            pltpu.VMEM((tiles, unit, unit), f32),
            pltpu.VMEM((total_ex, total_ex), f32),
            pltpu.VMEM((split, total_ex), low),
            pltpu.VMEM((split, total_ex), low),
            pltpu.VMEM((1, total_ex), f32),
            pltpu.VMEM((1, total_ex), f32),
            pltpu.VMEM((8, total_ex), f32),
            pltpu.VMEM((total_ex, 128), f32),
            pltpu.VMEM((batch * group_ex, total_ex), low),
            pltpu.VMEM((batch * group_ex, total_ex), low),
            pltpu.VMEM((batch * group_ex, total_ex), low),
            pltpu.VMEM((batch, ITERS, group_ex, group_ex), f32),
            pltpu.VMEM((groups // 2, group_ex, group_ex), f32),
            pltpu.VMEM((blocks, examples, group_ex), f32),
            dma((2 * slots,)), dma((2,)), dma((CHUNKS,)), dma((UNITS,)), dma, dma,
            dma((tiles,)), dma((tiles,)), dma, dma,
            dma((groups // 2 * blocks,)), dma((blocks,)),
        ],
        compiler_params=pltpu.CompilerParams(
            collective_id=0, has_side_effects=True, vmem_limit_bytes=67043328
        ),
    )(activations, out_grads, proj_act, proj_out)
    return scores * float(examples * groups)


def solution(mesh):
    in_specs = (P(("grp", "blk"), None), P(("grp", "blk"), None), P(), P())
    out_specs = P(("grp", "blk"), None)
    body = functools.partial(shards, mesh.shape["grp"], mesh.shape["blk"])
    return jax.shard_map(body, mesh=mesh, in_specs=in_specs, out_specs=out_specs, check_vma=False)
```

time: 57.3 us -> 52.4 us (0.914)
  Pallas kernels: 55.8 us -> 50.8 us
    pallas_call x1, Pallas kernels: 55.8 us -> 50.8 us  [shards(): pl.pallas_call(functools.partial(mix_kernel, groups, blocks, examples, ra...]
where the time goes in v2:
time: 52.4 us; the launch traced here: 52.2 us
  Pallas kernels  50.8 us (97%)
  other arithmetic  1.3 us (2%)
    pallas_call x1, Pallas kernels, shards(): pl.pallas_call(functools.partial(mix_kernel, groups, blocks, examples, ra...  50.8 us
    mul x1, other arithmetic, shards(): return scores * float(examples * groups)  1.3 us

profile of v2, /device:TPU:0, one launch (start us, length us, event | category | flops | bytes accessed | tf_op | source)
XLA Modules:
  0.0 52.2 jit_solution(6349071823529681838)
XLA Ops:
  0.0 50.8 %shard_map.46 = f32[16,128]{1,0:T(8,128)} custom-call(bf16[1024,3072]{1,0:T(8,128)(2,1)} %act_hbm.1, bf16[1024,3072]{1,0:T(8,128)(2,1)} %grad_hbm.1, bf16[3072,128]{1,0:T(8,128)(2,1)} %pact_hbm.1, bf16[3072,256]{1,0:T(8,128)(2,1)} %pout_hbm.1), custom_call_target="tpu_custom_call" | custom-call | tf_op jit(solution)/shard_map/pallas_call | solution.py:470
  50.9 1.3 %broadcast_multiply_fusion = f32[16,128]{1,0:T(8,128)} fusion(f32[16,128]{1,0:T(8,128)} %shard_map.46), kind=kLoop, calls=%fused_computation | loop fusion | flops 2048 | bytes 16384 | tf_op jit(solution)/shard_map/mul | solution.py:508

commit v3 on v2

--- a/solution.py
+++ b/solution.py
@@ -15,11 +15,10 @@
 CHUNKS = 2
 PARTS = 4
 AHEAD = 2
-UNITS = 4
 MESH = pl.DeviceIdType.MESH
 NT = (((1,), (1,)), ((), ()))
 TN = (((0,), (0,)), ((), ()))
-TILES = [(i, j) for i in range(UNITS) for j in range(i + 1)]
+TILES = [(i, j) for i in range(CHUNKS) for j in range(i + 1)]
 
 
 def mix_kernel(
@@ -31,12 +30,12 @@
 ):
     devices = groups * blocks
     planes = blocks // 2
-    near = planes // 2
+    far = planes // 2
     targets = 2 * blocks
     group_ex = examples * blocks
     total_ex = group_ex * groups
-    unit = total_ex // UNITS
-    span = recv.shape[3]
+    unit = total_ex // CHUNKS
+    span = recv.shape[2]
     ex_c = examples // CHUNKS
     core_groups = groups // 2
     grp, blk = lax.axis_index("grp"), lax.axis_index("blk")
@@ -55,7 +54,8 @@
         return lax.rem((source - target) * flip + planes, planes)
 
     def target_of(d):
-        rel = lax.rem(near + lax.div(d, 4), planes)
+        n = lax.div(d, 4)
+        rel = lax.rem(far - n + planes, planes)
         j = lax.rem(d, 4)
         side = lax.rem(grp + lax.div(j, 2), 2)
         pc = lax.rem(core + lax.rem(j, 2), 2)
@@ -121,24 +121,38 @@
                     product[:, h * 128:(h + 1) * 128])
 
     def narrow(chunk, slot):
+        squares = jnp.zeros((8, 128), jnp.float32)
         for r in range(ranks):
             rows = pl.ds(pl.multiple_of((slot * ranks + r) * ex_c, ex_c), ex_c)
             for h in range(wide.shape[0]):
                 low = wide[h, rows, :].astype(jnp.bfloat16)
                 feat[chunk, slot, r, :, h * 128:(h + 1) * 128] = low
                 back = low.astype(jnp.float32)
-                stat_acc[...] += jnp.sum((back * back).reshape(ex_c // 8, 8, 128), axis=0)
+                squares += jnp.sum((back * back).reshape(ex_c // 8, 8, 128), axis=0)
+        stat_acc[...] += squares
 
     def landing(chunk, pp):
-        rel = seen_from(plane, pp)
-        u = 2 * lax.div(rel, near) + chunk
-        at = (lax.rem(rel, near) * groups + grp) * 2 + core
-        return recv.at[u, :, pl.ds(pl.multiple_of(at * ex_c, ex_c), ex_c), :], u
+        at = (seen_from(plane, pp) * groups + grp) * 2 + core
+        return recv.at[:, pl.ds(pl.multiple_of(chunk * unit + at * ex_c, ex_c), ex_c), :]
 
     def either(side, pp, pc, local, remote):
         mine = jnp.logical_and(side * far_end == grp, 2 * pp + pc == blk)
         pl.when(mine)(local)
         pl.when(jnp.logical_not(mine))(remote)
+
+    def send_stat(d, c):
+        side, pp, pc = target_of(d)
+
+        def local():
+            pltpu.make_async_copy(stat_row, stats.at[me], t_recv).start()
+
+        def remote():
+            pltpu.make_async_remote_copy(
+                src_ref=stat_row, dst_ref=stats.at[me], send_sem=t_send, recv_sem=t_recv,
+                device_id=(side * far_end, 2 * pp + pc), device_id_type=MESH).start()
+
+        either(side, pp, pc, local, remote)
+        return c
 
     for chunk in range(CHUNKS):
         for k in range(parts_c):
@@ -146,43 +160,36 @@
         if chunk == 0:
             pl.semaphore_wait(barrier, devices - 1)
 
-        def send(d, c, chunk=chunk):
+        last_chunk = chunk == CHUNKS - 1
+        if last_chunk:
+            def settle_slot(slot, c, chunk=chunk):
+                narrow(chunk, slot)
+                return c
+
+            lax.fori_loop(0, targets, settle_slot, 0)
+            stat_row[...] = jnp.sum(stat_acc[...], axis=0, keepdims=True)
+            lax.fori_loop(0, targets, send_stat, 0)
+
+        def send(d, c, chunk=chunk, last_chunk=last_chunk):
             side, pp, pc = target_of(d)
             slot = (2 * pp + side) * 2 + pc
-            narrow(chunk, slot)
-            dst, u = landing(chunk, pp)
+            if not last_chunk:
+                narrow(chunk, slot)
+            dst = landing(chunk, pp)
 
             def local():
-                pltpu.make_async_copy(feat.at[chunk, slot], dst, f_recv.at[u]).start()
+                pltpu.make_async_copy(feat.at[chunk, slot], dst, f_recv.at[chunk]).start()
 
             def remote():
                 pltpu.make_async_remote_copy(
                     src_ref=feat.at[chunk, slot], dst_ref=dst,
-                    send_sem=f_send.at[chunk], recv_sem=f_recv.at[u],
+                    send_sem=f_send.at[chunk], recv_sem=f_recv.at[chunk],
                     device_id=(side * far_end, 2 * pp + pc), device_id_type=MESH).start()
 
             either(side, pp, pc, local, remote)
             return c
 
         lax.fori_loop(0, targets, send, 0)
-
-    stat_row[...] = jnp.sum(stat_acc[...], axis=0, keepdims=True)
-
-    def send_stat(d, c):
-        side, pp, pc = target_of(d)
-
-        def local():
-            pltpu.make_async_copy(stat_row, stats.at[me], t_recv).start()
-
-        def remote():
-            pltpu.make_async_remote_copy(
-                src_ref=stat_row, dst_ref=stats.at[me], send_sem=t_send, recv_sem=t_recv,
-                device_id=(side * far_end, 2 * pp + pc), device_id_type=MESH).start()
-
-        either(side, pp, pc, local, remote)
-        return c
-
-    lax.fori_loop(0, targets, send_stat, 0)
 
     ones = jnp.ones((8, span), jnp.bfloat16)
     norm = 1.0 / math.sqrt(width)
@@ -197,12 +204,13 @@
         return high, (v - high.astype(jnp.float32)).astype(jnp.bfloat16)
 
     def arrive(u):
-        pltpu.make_async_copy(recv.at[u], recv.at[u], f_recv.at[u]).wait()
-
-    def over_ranks(left, v):
+        rows = recv.at[:, pl.ds(u * unit, unit), :]
+        pltpu.make_async_copy(rows, rows, f_recv.at[u]).wait()
+
+    def over_ranks(left, right):
         total = None
         for r in range(ranks):
-            term = nt(left(r), recv[v, r])
+            term = nt(left(r), recv[r, right, :])
             total = term if total is None else total + term
         return total
 
@@ -210,7 +218,7 @@
         return slice(u * unit, (u + 1) * unit), slice(v * unit, (v + 1) * unit)
 
     def tile_copy(u, v):
-        t = u * (u + 1) // 2 + v
+        t = TILES.index((u, v))
         a, b = area(u, v)
         return pltpu.make_async_remote_copy(
             src_ref=full.at[a, b], dst_ref=land.at[t],
@@ -223,30 +231,22 @@
             device_id=partner, device_id_type=MESH)
 
     def rel_row(group, q, pc, ch):
-        rel = seen_from(q, plane)
-        u = 2 * lax.div(rel, near) + ch
-        return u * unit + ((lax.rem(rel, near) * groups + group) * 2 + pc) * ex_c
+        return ch * unit + ((seen_from(q, plane) * groups + group) * 2 + pc) * ex_c
+
+    step_sq = min(256, unit)
+
+    def squares_of(u, v):
+        return [
+            (slice(u * unit + i, u * unit + i + step_sq), slice(v * unit + j, v * unit + j + step_sq),
+             slice(i, i + step_sq), slice(j, j + step_sq))
+            for i in range(0, unit, step_sq) for j in range(0, unit, step_sq)]
 
     def own_work():
-        for u in range(UNITS):
-            arrive(u)
-            if u == 0:
-                pltpu.make_async_copy(stats, stats, t_recv).wait()
-            total = jnp.sum(jnp.sum(stats[...], axis=0), axis=1, keepdims=True)
-            shrink = 1.0 / (total + 1e-30)
-            for v in range(u + 1):
-                a, b = area(u, v)
-                full[a, b] = over_ranks(lambda r, u=u: recv[u, r], v)
-                tile_copy(u, v).start()
-            prow_part[:, u * unit:(u + 1) * unit] = over_ranks(lambda r: ones, u)[:1] * norm
-            if u == UNITS - 1:
-                prow_copy().start()
-            for v in range(u + 1):
-                t = u * (u + 1) // 2 + v
-                a, b = area(u, v)
-                tile_copy(u, v).wait_recv()
-                tile_copy(u, v).wait_send()
-                both = full[a, b] + land[t]
+        def settle(u, v):
+            tile_copy(u, v).wait_recv()
+            tile_copy(u, v).wait_send()
+            for a, b, i, j in squares_of(u, v):
+                both = full[a, b] + land[TILES.index((u, v)), i, j]
                 full[a, b] = both
                 if keep:
                     w_high[a, b], w_low[a, b] = halves(both * shrink)
@@ -255,6 +255,23 @@
                     full[b, a] = both
                     if keep:
                         w_high[b, a], w_low[b, a] = halves(both * shrink)
+
+        for u in range(CHUNKS):
+            arrive(u)
+            for v in range(u + 1):
+                for a, b, _, _ in squares_of(u, v):
+                    full[a, b] = over_ranks(lambda r, a=a: recv[r, a, :], b)
+                tile_copy(u, v).start()
+            here = slice(u * unit, (u + 1) * unit)
+            prow_part[:, here] = over_ranks(lambda r: ones, here)[:1] * norm
+            if u == CHUNKS - 1:
+                prow_copy().start()
+            if u == 0:
+                pltpu.make_async_copy(stats, stats, t_recv).wait()
+                total = jnp.sum(jnp.sum(stats[...], axis=0), axis=1, keepdims=True)
+                shrink = 1.0 / (total + 1e-30)
+            for v in range(u + 1):
+                settle(u, v)
         damping = damping_rate * total / (width * blocks)
         prow_copy().wait_recv()
         prow_copy().wait_send()
@@ -389,26 +406,27 @@
                     score = score + factors[k] * acc[n, k]
                 sc[first + n] = score
 
-                def send_score(d, c, n=first + n):
-                    b = lax.rem(blk + blocks // 2 + d, blocks)
-                    group = core * core_groups + n
-                    src = sc.at[n, pl.ds(pl.multiple_of(b * examples, examples), examples)]
-                    mine = jnp.logical_and(group == grp, b == blk)
-
-                    @pl.when(mine)
-                    def _():
-                        pltpu.make_async_copy(src, sc_land.at[block], o_recv.at[block]).start()
-
-                    @pl.when(jnp.logical_not(mine))
-                    def _():
-                        pltpu.make_async_remote_copy(
-                            src_ref=src, dst_ref=sc_land.at[block],
-                            send_sem=o_send.at[n * blocks + b], recv_sem=o_recv.at[block],
-                            device_id=(group, b), device_id_type=MESH).start()
-
-                    return c
-
-                lax.fori_loop(0, blocks, send_score, 0)
+        def send_score(d, c):
+            b = 2 * lax.div(d, 2 * core_groups) + lax.rem(d, 2)
+            n = lax.rem(lax.div(d, 2), core_groups)
+            group = core * core_groups + n
+            src = sc.at[n, pl.ds(pl.multiple_of(b * examples, examples), examples)]
+            mine = jnp.logical_and(group == grp, b == blk)
+
+            @pl.when(mine)
+            def _():
+                pltpu.make_async_copy(src, sc_land.at[block], o_recv.at[block]).start()
+
+            @pl.when(jnp.logical_not(mine))
+            def _():
+                pltpu.make_async_remote_copy(
+                    src_ref=src, dst_ref=sc_land.at[block],
+                    send_sem=o_send.at[n * blocks + b], recv_sem=o_recv.at[block],
+                    device_id=(group, b), device_id_type=MESH).start()
+
+            return c
+
+        lax.fori_loop(0, core_groups * blocks, send_score, 0)
 
     pl.when(is_owner)(own_work)
 
@@ -456,7 +474,7 @@
     group_ex, total_ex = examples * blocks, examples * devices
     ranks = rank // targets
     width = rank * span // blocks
-    unit = total_ex // UNITS
+    unit = total_ex // CHUNKS
     ex_c, rows_l = examples // CHUNKS, tokens // PARTS
     small = total_ex <= 1024
     slots = PARTS if small else AHEAD
@@ -479,7 +497,7 @@
             pltpu.VMEM((depth, span), low),
             pltpu.VMEM((span // 128, rank * ex_c, 128), f32),
             pltpu.VMEM((CHUNKS, targets, ranks, ex_c, span), low),
-            pltpu.VMEM((UNITS, ranks, unit, span), low),
+            pltpu.VMEM((ranks, total_ex, span), low),
             pltpu.VMEM((8, 128), f32),
             pltpu.VMEM((1, 128), f32),
             pltpu.VMEM((devices, 1, 128), f32),
@@ -497,7 +515,7 @@
             pltpu.VMEM((batch, ITERS, group_ex, group_ex), f32),
             pltpu.VMEM((groups // 2, group_ex, group_ex), f32),
             pltpu.VMEM((blocks, examples, group_ex), f32),
-            dma((2 * slots,)), dma((2,)), dma((CHUNKS,)), dma((UNITS,)), dma, dma,
+            dma((2 * slots,)), dma((2,)), dma((CHUNKS,)), dma((CHUNKS,)), dma, dma,
             dma((tiles,)), dma((tiles,)), dma, dma,
             dma((groups // 2 * blocks,)), dma((blocks,)),
         ],

time: 52.4 us -> 46.2 us (0.88)
  Pallas kernels: 50.8 us -> 44.7 us
    pallas_call x1, Pallas kernels: 50.8 us -> 44.7 us  [shards(): pl.pallas_call(functools.partial(mix_kernel, groups, blocks, examples, ra...]
where the time goes in v3:
time: 46.2 us; the launch traced here: 46 us
  Pallas kernels  44.7 us (97%)
  other arithmetic  1.3 us (3%)
    pallas_call x1, Pallas kernels, shards(): pl.pallas_call(functools.partial(mix_kernel, groups, blocks, examples, ra...  44.7 us
    mul x1, other arithmetic, shards(): return scores * float(examples * groups)  1.3 us

profile of v3, /device:TPU:0, one launch (start us, length us, event | category | flops | bytes accessed | tf_op | source)
XLA Modules:
  0.0 46.0 jit_solution(10133162576277977848)
XLA Ops:
  0.0 44.7 %shard_map.46 = f32[16,128]{1,0:T(8,128)} custom-call(bf16[1024,3072]{1,0:T(8,128)(2,1)} %act_hbm.1, bf16[1024,3072]{1,0:T(8,128)(2,1)} %grad_hbm.1, bf16[3072,128]{1,0:T(8,128)(2,1)} %pact_hbm.1, bf16[3072,256]{1,0:T(8,128)(2,1)} %pout_hbm.1), custom_call_target="tpu_custom_call" | custom-call | tf_op jit(solution)/shard_map/pallas_call | solution.py:488
  44.7 1.3 %broadcast_multiply_fusion = f32[16,128]{1,0:T(8,128)} fusion(f32[16,128]{1,0:T(8,128)} %shard_map.46), kind=kLoop, calls=%fused_computation | loop fusion | flops 2048 | bytes 16384 | tf_op jit(solution)/shard_map/mul | solution.py:526

commit v4 on v3

--- a/solution.py
+++ b/solution.py
@@ -520,9 +520,11 @@
             dma((groups // 2 * blocks,)), dma((blocks,)),
         ],
         compiler_params=pltpu.CompilerParams(
-            collective_id=0, has_side_effects=True, vmem_limit_bytes=67043328
+            collective_id=0, has_side_effects=True,
+            vmem_limit_bytes=(40 << 20) if small else 67043328,
         ),
-    )(activations, out_grads, proj_act, proj_out)
+    )(*[pltpu.with_memory_space_constraint(v, pltpu.HBM)
+        for v in (activations, out_grads, proj_act, proj_out)])
     return scores * float(examples * groups)
 
 

time: 46.2 us -> 44.8 us (0.970)
  other arithmetic: 1.3 us -> 0.6 us
  Pallas kernels: 44.7 us -> 44.1 us
    mul x1, other arithmetic: 1.3 us -> 0.6 us  [shards(): return scores * float(examples * groups)]
    pallas_call x1, Pallas kernels: 44.7 us -> 44.1 us  [shards(): pl.pallas_call(functools.partial(mix_kernel, groups, blocks, examples, ra...]
where the time goes in v4:
time: 44.8 us; the launch traced here: 44.7 us
  Pallas kernels  44.1 us (98%)
  other arithmetic  0.6 us (1%)
    pallas_call x1, Pallas kernels, shards(): pl.pallas_call(functools.partial(mix_kernel, groups, blocks, examples, ra...  44.1 us

profile of v4, /device:TPU:0, one launch (start us, length us, event | category | flops | bytes accessed | tf_op | source)
XLA Modules:
  0.0 44.7 jit_solution(12593026798968705096)
XLA Ops:
  0.0 44.1 %shard_map.46 = f32[16,128]{1,0:T(8,128)S(1)} custom-call(bf16[1024,3072]{1,0:T(8,128)(2,1)} %act_hbm.1, bf16[1024,3072]{1,0:T(8,128)(2,1)} %grad_hbm.1, bf16[3072,128]{1,0:T(8,128)(2,1)} %pact_hbm.1, bf16[3072,256]{1,0:T(8,128)(2,1)} %pout_hbm.1), custom_call_target="tpu_custom_call" | custom-call | tf_op jit(solution)/shard_map/pallas_call | solution.py:488
  44.1 0.6 %broadcast_multiply_fusion = f32[16,128]{1,0:T(8,128)} fusion(f32[16,128]{1,0:T(8,128)S(1)} %shard_map.46), kind=kLoop, calls=%fused_computation | loop fusion | flops 2048 | bytes 16384 | tf_op jit(solution)/shard_map/mul | solution.py:528

commit v5 on v4

--- a/solution.py
+++ b/solution.py
@@ -191,7 +191,7 @@
 
         lax.fori_loop(0, targets, send, 0)
 
-    ones = jnp.ones((8, span), jnp.bfloat16)
+    ones = jnp.ones((16, span), jnp.bfloat16)
     norm = 1.0 / math.sqrt(width)
     partner = (grp, blk + 1 - 2 * core)
     pieces = [(q, pc, ch) for q in range(planes) for pc in range(2) for ch in range(CHUNKS)]
@@ -242,6 +242,28 @@
             for i in range(0, unit, step_sq) for j in range(0, unit, step_sq)]
 
     def own_work():
+        def spots(first):
+            for n in range(batch):
+                group = core * core_groups + first + n
+                for m in range(0, len(pieces), 2):
+                    at, to = rel_row(group, *pieces[m]), rel_row(group, *pieces[m + 1])
+                    here = slice(n * group_ex + m * ex_c, n * group_ex + (m + 2) * ex_c)
+                    lane = lax.broadcasted_iota(jnp.int32, (2 * ex_c, total_ex), 1)
+                    sub = lax.broadcasted_iota(jnp.int32, (2 * ex_c, total_ex), 0)
+                    spot = jnp.where(sub < ex_c, at + sub, to + sub - ex_c)
+                    pick[here, :] = jnp.where(spot == lane, 1.0, 0.0).astype(jnp.bfloat16)
+
+        def gather(first):
+            for n in range(batch):
+                group = core * core_groups + first + n
+                for m in range(0, len(pieces), 2):
+                    at, to = rel_row(group, *pieces[m]), rel_row(group, *pieces[m + 1])
+                    at, to = pl.multiple_of(at, ex_c), pl.multiple_of(to, ex_c)
+                    y = jnp.concatenate(
+                        [full[pl.ds(at, ex_c), :], full[pl.ds(to, ex_c), :]], axis=0) * shrink
+                    here = slice(n * group_ex + m * ex_c, n * group_ex + (m + 2) * ex_c)
+                    y_high[here, :], y_low[here, :] = halves(y)
+
         def settle(u, v):
             tile_copy(u, v).wait_recv()
             tile_copy(u, v).wait_send()
@@ -256,14 +278,22 @@
                     if keep:
                         w_high[b, a], w_low[b, a] = halves(both * shrink)
 
+        spots(0)
         for u in range(CHUNKS):
             arrive(u)
             for v in range(u + 1):
-                for a, b, _, _ in squares_of(u, v):
-                    full[a, b] = over_ranks(lambda r, a=a: recv[r, a, :], b)
+                for a, b, i, j in squares_of(u, v):
+                    summed = u == v and i.start == 0
+
+                    def left(r, a=a, summed=summed):
+                        rows = recv[r, a, :]
+                        return jnp.concatenate([rows, ones], axis=0) if summed else rows
+
+                    found = over_ranks(left, b)
+                    full[a, b] = found[:step_sq]
+                    if summed:
+                        prow_part[:, b] = found[step_sq:step_sq + 1] * norm
                 tile_copy(u, v).start()
-            here = slice(u * unit, (u + 1) * unit)
-            prow_part[:, here] = over_ranks(lambda r: ones, here)[:1] * norm
             if u == CHUNKS - 1:
                 prow_copy().start()
             if u == 0:
@@ -303,40 +333,27 @@
 
         step_ex = min(256, total_ex)
 
-        def prepare(first):
-            for n in range(batch):
-                group = core * core_groups + first + n
-                for m in range(0, len(pieces), 2):
-                    at, to = rel_row(group, *pieces[m]), rel_row(group, *pieces[m + 1])
-                    at, to = pl.multiple_of(at, ex_c), pl.multiple_of(to, ex_c)
-                    y = jnp.concatenate(
-                        [full[pl.ds(at, ex_c), :], full[pl.ds(to, ex_c), :]], axis=0) * shrink
-                    here = slice(n * group_ex + m * ex_c, n * group_ex + (m + 2) * ex_c)
-                    y_high[here, :], y_low[here, :] = halves(y)
-                    lane = lax.broadcasted_iota(jnp.int32, (2 * ex_c, total_ex), 1)
-                    sub = lax.broadcasted_iota(jnp.int32, (2 * ex_c, total_ex), 0)
-                    spot = jnp.where(sub < ex_c, at + sub, to + sub - ex_c)
-                    pick[here, :] = jnp.where(spot == lane, 1.0, 0.0).astype(jnp.bfloat16)
-
         def powers(at, fresh):
             yh, yl = y_high[...], y_low[...]
             if keep:
                 wh, wl = w_high[at, :], w_low[at, :]
             else:
                 wh, wl = halves(full[at, :] * shrink)
-            vh, vl = halves(nt(yh, wh) + (nt(yh, wl) + nt(yl, wh)))
+            count = yh.shape[0]
+            stacked = nt(jnp.concatenate([yh, yl], axis=0), wh)
+            vh, vl = halves(stacked[:count] + (stacked[count:] + nt(yh, wl)))
+            g = group_ex
             for n in range(batch):
-                here = slice(n * group_ex, (n + 1) * group_ex)
+                here = slice(n * g, (n + 1) * g)
                 ah, al, ph = y_high[here, at], y_low[here, at], pick[here, at]
                 bh, bl = vh[here], vl[here]
-                right = jnp.concatenate([ah, ph], axis=0)
-                one = nt(ah, right) + nt(al, right)
-                one_low = nt(ah, al)
-                both_h = jnp.concatenate([ah, bh], axis=0)
-                both_l = jnp.concatenate([al, bl], axis=0)
-                two = nt(bh, both_h) + (nt(bh, both_l) + nt(bl, both_h))
-                terms = (one[:, group_ex:], one[:, :group_ex] + one_low,
-                         two[:, :group_ex], two[:, group_ex:])
+                one = nt(jnp.concatenate([ah, al], axis=0), jnp.concatenate([ah, ph], axis=0))
+                two = nt(jnp.concatenate([bh, bl], axis=0), jnp.concatenate([ah, bh], axis=0))
+                low = nt(jnp.concatenate([ah, bh], axis=0), jnp.concatenate([al, bl], axis=0))
+                terms = (one[:g, g:] + one[g:, g:],
+                         one[:g, :g] + (one[g:, :g] + low[:g, :g]),
+                         two[:g, :g] + (two[g:, :g] + low[g:, :g]),
+                         two[:g, g:] + (two[g:, g:] + low[g:, g:]))
                 for k, term in enumerate(terms):
                     acc[n, k] = term if fresh else acc[n, k] + term
 
@@ -353,7 +370,7 @@
 
                 lax.fori_loop(0, total_ex // step_ex, one_step, 0)
 
-        prepare(0)
+        gather(0)
         multiply()
         values = row[:1, :]
         top = None
@@ -383,8 +400,9 @@
         solution_poly = [one]
         residual = plus([one], shifted(direction), -sig)
         for sweep in range(1, ITERS):
-            momentum = 0.5 * (rho * sig) ** 2 if sweep == 1 else (0.5 * rho * sig) ** 2
-            sig = 1.0 / (1.0 - momentum / sig)
+            pull = (0.5 if sweep == 1 else 0.25) * rho * rho * sig
+            momentum = pull * sig
+            sig = 1.0 / (1.0 - pull)
             direction = plus(residual, direction, momentum)
             solution_poly = plus(solution_poly, direction, sig)
             if sweep + 1 < ITERS:
@@ -398,7 +416,8 @@
 
         for first in range(0, core_groups, batch):
             if first:
-                prepare(first)
+                spots(first)
+                gather(first)
                 multiply()
             for n in range(batch):
                 score = factors[0] * acc[n, 0]

time: 44.8 us -> 44.4 us (level)
  Pallas kernels: 44.1 us -> 43.6 us
where the time goes in v5:
time: 44.4 us; the launch traced here: 44.2 us
  Pallas kernels  43.6 us (98%)
  other arithmetic  0.6 us (1%)
    pallas_call x1, Pallas kernels, shards(): pl.pallas_call(functools.partial(mix_kernel, groups, blocks, examples, ra...  43.6 us

profile of v5, /device:TPU:0, one launch (start us, length us, event | category | flops | bytes accessed | tf_op | source)
XLA Modules:
  0.0 44.2 jit_solution(18427848023162418632)
XLA Ops:
  0.0 43.6 %shard_map.46 = f32[16,128]{1,0:T(8,128)S(1)} custom-call(bf16[1024,3072]{1,0:T(8,128)(2,1)} %act_hbm.1, bf16[1024,3072]{1,0:T(8,128)(2,1)} %grad_hbm.1, bf16[3072,128]{1,0:T(8,128)(2,1)} %pact_hbm.1, bf16[3072,256]{1,0:T(8,128)(2,1)} %pout_hbm.1), custom_call_target="tpu_custom_call" | custom-call | tf_op jit(solution)/shard_map/pallas_call | solution.py:507
  43.6 0.6 %broadcast_multiply_fusion = f32[16,128]{1,0:T(8,128)} fusion(f32[16,128]{1,0:T(8,128)S(1)} %shard_map.46), kind=kLoop, calls=%fused_computation | loop fusion | flops 2048 | bytes 16384 | tf_op jit(solution)/shard_map/mul | solution.py:547
